TPU v7x, 128 devices: a whole 4x4x4 slice. The times are simulated.
128 devices in a mesh: fsdp: 16 (over x_hi, y, core), loop: 8 (over z, x_lo).
Axes of the slice: x: 4 (x_hi: 2, x_lo: 2; x = x_hi * 2 + x_lo), y: 4, z: 4, core: 2. Of those that a mesh axis runs over, the one named last changes fastest.
Arguments:
- iterate: bfloat16 [8, 7168, 2048], P(None, 'fsdp', 'loop'), may hold values from -0.0625 to 0.0625
- expert_order: int32 [8], replicated, may hold values from 0 to 7, each once
Outputs:
- update: bfloat16 [8, 7168, 2048], P(None, 'fsdp', 'loop')
Inputs may be any that keep to these rules, and one draw needn't show every extreme that they name: `expert_order`: each value names a different expert.
All inputs are finite; a program needn't handle non-finite values.
Results may differ from a plain program's by a relative error of at most 0.006.
Values may be sent and summed in bfloat16 or wider, within the bound.
A program may use at most 128 MiB of HBM per device.

v0:
```python
import jax
import jax.numpy as jnp
from jax import lax
from jax.sharding import PartitionSpec as P

D = 7168
coef_linear = 3.4445
coef_cubic = -4.775


def half_step(left, right):
    factor = 0.2 * D**0.5
    partial_gram = jnp.einsum("eic,eik->eck", left, right, preferred_element_type=jnp.float32)
    summed = lax.psum(partial_gram, "fsdp")
    gram_block = summed.astype(jnp.bfloat16)
    product = jnp.einsum("eik,eck->eic", right, gram_block, preferred_element_type=jnp.float32)
    result = factor * (coef_linear * left.astype(jnp.float32) + coef_cubic * product)
    return result.astype(jnp.bfloat16)


def body(iterate, expert_order):
    chosen = jnp.take(iterate, expert_order, axis=0)
    gathered = lax.all_gather(chosen, "loop", axis=2, tiled=True)
    return half_step(chosen, gathered)


def solution(mesh):
    placed = (P(None, "fsdp", "loop"), P())
    return jax.shard_map(
        body, mesh=mesh, in_specs=placed, out_specs=P(None, "fsdp", "loop"), check_vma=False
    )
```

profile of v0, /device:TPU:6, one launch (start us, length us, event | category | flops | bytes accessed | tf_op | source)
XLA Modules:
  0.0 530.2 jit_solution(17105883795488496706)
XLA Ops:
  6.5 0.0 copy-start
  6.5 0.0 all-gather.2.cloned.1.call-start
  6.5 0.8 compare_and_fusion
  7.3 0.7 compare_select_fusion
  8.0 0.0 copy-done
  8.1 1.9 gather_fusion
  9.9 3.0 broadcast_select_fusion
  12.9 0.0 all-gather.2.cloned.1.call-update
  12.9 288.9 %all-gather.2.cloned.1.call-done = bf16[8,448,2048]{2,1,0:T(8,128)(2,1)} async-done(((bf16[8,448,256]{2,1,0:T(8,128)(2,1)}), bf16[8,448,2048]{2,1,0:T(8,128)(2,1)}) %all-gather.2.cloned.1.call-update) | async-done | bytes 14680080 | tf_op jit(solution)/shard_map/all_gather | solution.py:23
  301.8 16.0 %fusion.4 = f32[8,256,2048]{2,1,0:T(8,128)} fusion(bf16[8,448,256]{2,1,0:T(8,128)(2,1)} %broadcast_select_fusion, bf16[8,448,2048]{2,1,0:T(8,128)(2,1)} %all-gather.2.cloned.1.call-done), kind=kOutput, calls=%fused_computation.8 | convolution fusion | flops 3758096384 | bytes 33292288 | tf_op jit(solution)/shard_map/eic,eik->eck/dot_general | solution.py:13
  317.8 193.1 %all-reduce.1 = bf16[8,256,2048]{2,1,0:T(8,128)(2,1)} all-reduce(f32[8,256,2048]{2,1,0:T(8,128)} %fusion.4), channel_id=1, replica_groups=mesh['fsdp'=16,'loop'=8] {'fsdp'}, use_global_device_ids=true, to_apply=%region_0.1 | all-reduce | flops 4194304 | bytes 25165824 | tf_op jit(solution)/shard_map/psum | solution.py:14
  510.9 12.5 %multiply_convert_fusion = bf16[8,448,256]{2,1,0:T(8,128)(2,1)} fusion(bf16[8,448,256]{2,1,0:T(8,128)(2,1)} %broadcast_select_fusion, bf16[8,448,2048]{2,1,0:T(8,128)(2,1)} %all-gather.2.cloned.1.call-done, bf16[8,256,2048]{2,1,0:T(8,128)(2,1)} %all-reduce.1), kind=kOutput, calls=%fused_computation.3 | convolution fusion | flops 3763601408 | bytes 26738688 | tf_op jit(solution)/shard_map/eik,eck->eic/dot_general | solution.py:16
  (1 shorter events, 0.0 us)
Async XLA Ops:
  6.5 1.5 copy-start
  6.5 295.3 %all-gather.2.cloned.1.call-start = ((), (), s32[]{:S(2)}) async-start(), calls=%async_computation | async-start | bytes 16515072 | tf_op jit(solution)/shard_map/all_gather | solution.py:23
Sparse Core Ops, SparseCore 0:
  13.1 288.6 all-gather.1
where the time goes:
time: 530 us
  waiting for transfers between devices  289 us (55%)
  blocking collectives  193 us (36%)
  matrix products  28.5 us (5%)
  between operations  13.4 us (3%)
    all_gather x1, waiting for transfers between devices, body(): gathered = lax.all_gather(chosen, 'loop', axis=2, tiled=True)  289 us
    psum x1, blocking collectives, half_step(): summed = lax.psum(partial_gram, 'fsdp')  193 us
    dot_general x1, matrix products, half_step(): jnp.einsum('eic,eik->eck', left, right, preferred_element_type=jnp.float32)  16 us
    dot_general x1, matrix products, half_step(): jnp.einsum('eik,eck->eic', right, gram_block, preferred_element_type=jnp....  12.5 us
  transfers between devices with their start and end apart: 1, of which 1 were waited for; matrix products, arithmetic and copies ran while one was open for 0% of the time, Pallas kernels for 0%

commit v1 on v0

--- a/solution.py
+++ b/solution.py
@@ -20,7 +20,9 @@
 
 def body(iterate, expert_order):
     chosen = jnp.take(iterate, expert_order, axis=0)
-    gathered = lax.all_gather(chosen, "loop", axis=2, tiled=True)
+    gathered = jnp.concatenate(
+        lax.all_to_all(jnp.stack([chosen] * lax.axis_size("loop")), "loop", 0, 0), axis=2
+    )
     return half_step(chosen, gathered)
 
 

time: 530 us -> 403 us (0.76)
  waiting for transfers between devices: 289 us -> 0 us
  blocking collectives: 193 us -> 362 us
  between operations: 13.4 us -> 0.03 us
  local copies, waits for them, and re-layouts: 1.94 us -> 10.5 us
    all_gather x1 -> x0, waiting for transfers between devices: 289 us -> none  [body(): gathered = lax.all_gather(chosen, 'loop', axis=2, tiled=True)]
    all_to_all x0 -> x1, blocking collectives: none -> 169 us  [body(): lax.all_to_all(jnp.stack([chosen] * lax.axis_size('loop')), 'loop', 0, 0)]
    reshape x0 -> x1, local copies, waits for them, and re-layouts: none -> 6.72 us  [body(): jnp.concatenate(lax.all_to_all(jnp.stack([chosen] * lax.axis_size('loop')...]
  transfers between devices with their start and end apart: 1 -> 0, of which waited for: 1 -> 0; matrix products, arithmetic and copies ran while one was open for 0% -> 0% of each run, Pallas kernels for 0% -> 0%
where the time goes in v1:
time: 403 us; the launch traced here: 402 us
  blocking collectives  362 us (90%)
  matrix products  25.8 us (6%)
  local copies, waits for them, and re-layouts  10.5 us (3%)
    psum x1, blocking collectives, half_step(): summed = lax.psum(partial_gram, 'fsdp')  193 us
    all_to_all x1, blocking collectives, body(): lax.all_to_all(jnp.stack([chosen] * lax.axis_size('loop')), 'loop', 0, 0)  169 us
    dot_general x1, matrix products, half_step(): jnp.einsum('eic,eik->eck', left, right, preferred_element_type=jnp.float32)  13.3 us
    dot_general x1, matrix products, half_step(): jnp.einsum('eik,eck->eic', right, gram_block, preferred_element_type=jnp....  12.5 us

profile of v1, /device:TPU:6, one launch (start us, length us, event | category | flops | bytes accessed | tf_op | source)
XLA Modules:
  0.0 401.9 jit_solution(2808952853451094958)
XLA Ops:
  0.0 0.0 copy-start
  0.0 0.8 compare_and_fusion
  0.8 0.7 compare_select_fusion
  1.5 0.1 copy-done
  1.5 1.9 gather_fusion
  3.4 1.7 broadcast_select_fusion
  5.2 0.0 copy-start.2
  5.2 1.9 stack.2
  7.0 169.2 %all_to_all.5 = bf16[8,8,448,256]{3,2,1,0:T(8,128)(2,1)S(1)} all-to-all(bf16[8,8,448,256]{3,2,1,0:T(8,128)(2,1)S(1)} %stack.2), channel_id=1, replica_groups=mesh['fsdp'=16,'loop'=8] {'loop'}, dimensions={0} | all-to-all | bytes 29360128 | tf_op jit(solution)/shard_map/all_to_all | solution.py:24
  176.2 6.7 %copy.4 = bf16[8,8,56,8,256]{4,3,0,2,1:T(8,128)(2,1)} copy(bf16[8,8,56,8,256]{4,3,2,1,0:T(8,128)(2,1)S(1)} %bitcast.7) | data formatting | bytes 29360128 | tf_op jit(solution)/shard_map/reshape | solution.py:23
  182.9 0.0 copy-done.2
  182.9 13.3 %fusion.4 = f32[8,256,2048]{2,1,0:T(8,128)} fusion(bf16[8,448,256]{2,1,0:T(8,128)(2,1)S(1)} %broadcast_select_fusion, bf16[8,448,2048]{2,1,0:T(8,128)(2,1)} %bitcast.8), kind=kOutput, calls=%fused_computation.8 | convolution fusion | flops 3758096384 | bytes 33292288 | tf_op jit(solution)/shard_map/eic,eik->eck/dot_general | solution.py:13
  196.3 193.1 %all-reduce.1 = bf16[8,256,2048]{2,1,0:T(8,128)(2,1)} all-reduce(f32[8,256,2048]{2,1,0:T(8,128)} %fusion.4), channel_id=1, replica_groups=mesh['fsdp'=16,'loop'=8] {'fsdp'}, use_global_device_ids=true, to_apply=%region_0.1 | all-reduce | flops 4194304 | bytes 25165824 | tf_op jit(solution)/shard_map/psum | solution.py:14
  389.4 0.0 copy-start.1
  389.4 12.5 %multiply_convert_fusion = bf16[8,448,256]{2,1,0:T(8,128)(2,1)} fusion(bf16[8,448,256]{2,1,0:T(8,128)(2,1)} %copy-done.2, bf16[8,448,2048]{2,1,0:T(8,128)(2,1)} %bitcast.9, bf16[8,256,2048]{2,1,0:T(8,128)(2,1)} %all-reduce.1), kind=kOutput, calls=%fused_computation.3 | convolution fusion | flops 3763601408 | bytes 26738688 | tf_op jit(solution)/shard_map/eik,eck->eic/dot_general | solution.py:16
  401.9 0.0 copy-done.1
  (1 shorter events, 0.0 us)
Async XLA Ops:
  0.0 1.5 copy-start
  5.2 177.8 %copy-start.2 = (bf16[8,448,256]{2,1,0:T(8,128)(2,1)}, bf16[8,448,256]{2,1,0:T(8,128)(2,1)S(1)}, u32[]{:S(2)}) copy-start(bf16[8,448,256]{2,1,0:T(8,128)(2,1)S(1)} %broadcast_select_fusion) | copy-start | bytes 5505028
  389.4 12.5 %copy-start.1 = (bf16[8,448,256]{2,1,0:T(8,128)(2,1)S(1)}, bf16[8,448,256]{2,1,0:T(8,128)(2,1)}, u32[]{:S(2)}) copy-start(bf16[8,448,256]{2,1,0:T(8,128)(2,1)} %param.2) | copy-start | bytes 5505028
